TPU v7x, 512 devices: a whole 4x8x8 slice. The times are simulated.
512 devices in a mesh: ctx: 64 (over z, y_lo, core), fsdp: 8 (over y_hi, x).
Axes of the slice: x: 4, y: 8 (y_hi: 2, y_lo: 4; y = y_hi * 4 + y_lo), z: 8, core: 2. Of those that a mesh axis runs over, the one named last changes fastest.
Arguments:
- tokens: bfloat16 [8192, 4096], P('ctx', 'fsdp'), may hold values from -130 to 130, as said below
- w_query: bfloat16 [4096, 4096], P('ctx', 'fsdp'), may hold values from -0.09375 to 0.09375
- key_matrix: bfloat16 [4096, 1024], P('ctx', 'fsdp'), may hold values from -0.09375 to 0.09375
- value_matrix: bfloat16 [4096, 1024], P('ctx', 'fsdp'), may hold values from -0.09375 to 0.09375
- w_out: bfloat16 [4096, 4096], P('fsdp', 'ctx'), may hold values from -0.75 to 0.75
Outputs:
- mixed: bfloat16 [8192, 4096], P('ctx', 'fsdp')
Inputs may be any that keep to these rules, and one draw needn't show every extreme that they name: `tokens`: no structure of the entries is promised.
All inputs are finite; a program needn't handle non-finite values.
Results may differ from a plain program's by a relative error of at most 0.014.
The roundings to bfloat16 on the way count: a program that leaves them out, or rounds other values in their place, can miss the bound.
Values may be sent and summed in bfloat16 or wider, within the bound.
A program may use at most 64 MiB of HBM per device.

v0:
```python
import math
import jax
import jax.numpy as jnp
from jax import lax
from jax.sharding import PartitionSpec as P

HEAD_SIZE = 128


def rotate_heads(values, positions):
    tok_count = values.shape[0]
    head_count = values.shape[1] // HEAD_SIZE
    half_dim = HEAD_SIZE // 2
    inverse_freq = jnp.power(
        jnp.float32(500000.0), -jnp.arange(half_dim, dtype=jnp.float32) * 2.0 / HEAD_SIZE
    )
    angles = positions.astype(jnp.float32)[:, None] * inverse_freq[None, :]
    cosine = jnp.cos(angles)[:, None, :]
    sine_table = jnp.sin(angles)[:, None, :]
    shaped = values.reshape(tok_count, head_count, HEAD_SIZE)
    first_half = shaped[:, :, :half_dim]
    second = shaped[:, :, half_dim:]
    turned = jnp.concatenate(
        [first_half * cosine - second * sine_table, second * cosine + first_half * sine_table],
        axis=2,
    )
    return turned.reshape(tok_count, head_count * HEAD_SIZE).astype(jnp.bfloat16)


def body(tokens, w_query, key_matrix, value_matrix, w_out):
    features = lax.all_gather(tokens, "fsdp", axis=1, tiled=True)
    tok_count = features.shape[0]
    positions = lax.axis_index("ctx") * tok_count + jnp.arange(tok_count, dtype=jnp.int32)

    def add_rows(weight_piece):
        return jnp.dot(features, weight_piece, preferred_element_type=jnp.float32)

    query_sum = add_rows(lax.all_gather(w_query, "ctx", axis=0, tiled=True))
    key_sum = add_rows(lax.all_gather(key_matrix, "ctx", axis=0, tiled=True))
    value_sum = add_rows(lax.all_gather(value_matrix, "ctx", axis=0, tiled=True))
    queries = rotate_heads(query_sum, positions)
    projected_keys = rotate_heads(key_sum, positions)
    projected_values = value_sum.astype(jnp.bfloat16)
    kv_heads = projected_keys.shape[1] // HEAD_SIZE
    queries_per_group = queries.shape[1] // projected_keys.shape[1]
    stacked = (
        queries.reshape(tok_count, kv_heads, queries_per_group, HEAD_SIZE)
        .transpose(1, 2, 0, 3)
        .reshape(kv_heads, queries_per_group * tok_count, HEAD_SIZE)
    )
    query_pos = jnp.tile(positions, queries_per_group)
    score_scale = 1.0 / math.sqrt(HEAD_SIZE)

    def update(attn_state, key_block, value_block, key_start):
        row_max, row_total, accum = attn_state
        block_rows = key_block.shape[0]
        key_heads = key_block.reshape(block_rows, kv_heads, HEAD_SIZE)
        value_heads = value_block.reshape(block_rows, kv_heads, HEAD_SIZE)
        scores = (
            jnp.einsum("gqd,kgd->gqk", stacked, key_heads, preferred_element_type=jnp.float32)
            * score_scale
        )
        key_pos = key_start + jnp.arange(block_rows, dtype=jnp.int32)
        allowed = (key_pos[None, :] <= query_pos[:, None])[None]
        masked = jnp.where(allowed, scores, jnp.float32(-1e30))
        new_max = jnp.maximum(row_max, jnp.max(masked, axis=2))
        exp_weights = jnp.where(allowed, jnp.exp(masked - new_max[:, :, None]), jnp.float32(0.0))
        factor = jnp.exp(row_max - new_max)
        row_total = row_total * factor + jnp.sum(exp_weights, axis=2)
        accum = accum * factor[:, :, None] + jnp.einsum(
            "gqk,kgd->gqd",
            exp_weights.astype(jnp.bfloat16),
            value_heads,
            preferred_element_type=jnp.float32,
        )
        return (new_max, row_total, accum)

    query_rows = queries_per_group * tok_count
    initial = (
        jnp.full((kv_heads, query_rows), -1e30, jnp.float32),
        jnp.zeros((kv_heads, query_rows), jnp.float32),
        jnp.zeros((kv_heads, query_rows, HEAD_SIZE), jnp.float32),
    )
    key_piece = lax.all_gather(projected_keys, "ctx", axis=0, tiled=True)
    value_piece = lax.all_gather(projected_values, "ctx", axis=0, tiled=True)
    block_rows = min(tok_count, key_piece.shape[0])
    block_count = key_piece.shape[0] // block_rows

    def advance(block_index, carried):
        key_start = block_index * block_rows
        key_block = lax.dynamic_slice_in_dim(key_piece, block_index * block_rows, block_rows, 0)
        value_block = lax.dynamic_slice_in_dim(value_piece, block_index * block_rows, block_rows, 0)
        return update(carried, key_block, value_block, key_start)

    row_max, row_total, accum = lax.fori_loop(0, block_count, advance, initial)
    normed = accum / row_total[:, :, None]
    attn_out = (
        normed.reshape(kv_heads, queries_per_group, tok_count, HEAD_SIZE)
        .transpose(2, 0, 1, 3)
        .reshape(tok_count, kv_heads * queries_per_group * HEAD_SIZE)
        .astype(jnp.bfloat16)
    )
    partial_out = jnp.dot(
        attn_out,
        lax.all_gather(w_out, "ctx", axis=1, tiled=True),
        preferred_element_type=jnp.float32,
    )
    return lax.psum_scatter(
        partial_out.astype(jnp.bfloat16), "fsdp", scatter_dimension=1, tiled=True
    )


def solution(mesh):
    in_specs = (
        P("ctx", "fsdp"),
        P("ctx", "fsdp"),
        P("ctx", "fsdp"),
        P("ctx", "fsdp"),
        P("fsdp", "ctx"),
    )
    out_specs = P("ctx", "fsdp")
    return jax.shard_map(body, mesh=mesh, in_specs=in_specs, out_specs=out_specs, check_vma=False)
```

profile of v0, /device:TPU:2, one launch (start us, length us, event | category | flops | bytes accessed | tf_op | source)
XLA Modules:
  0.0 912.1 jit_solution(4390556370071659170)
XLA Ops:
  9.4 69.6 %all-gather.9.cloned.1.call-done = bf16[128,4096]{1,0:T(8,128)(2,1)} async-done(((bf16[128,512]{1,0:T(8,128)(2,1)}), bf16[128,4096]{1,0:T(8,128)(2,1)}) %all-gather.9.cloned.1.call-update) | async-done | bytes 1048592 | tf_op jit(solution)/shard_map/all_gather | solution.py:31
  79.0 117.3 %all-gather.11.cloned.1.call-done = bf16[4096,128]{1,0:T(8,128)(2,1)} async-done(((bf16[64,128]{1,0:T(8,128)(2,1)}), bf16[4096,128]{1,0:T(8,128)(2,1)}) %all-gather.11.cloned.1.call-update) | async-done | bytes 1048592 | tf_op jit(solution)/shard_map/all_gather | solution.py:39
  196.3 2.1 convolution_bitcast_fusion.1
  199.3 114.5 %all-gather.15.cloned.1.call-done = bf16[4096,128]{1,0:T(8,128)(2,1)} async-done(((bf16[64,128]{1,0:T(8,128)(2,1)}), bf16[4096,128]{1,0:T(8,128)(2,1)}) %all-gather.15.cloned.1.call-update) | async-done | bytes 1048592 | tf_op jit(solution)/shard_map/all_gather | solution.py:40
  313.7 2.6 convolution_convert_fusion.1
  317.5 116.0 %all-gather.13.cloned.1.call-done = bf16[4096,512]{1,0:T(8,128)(2,1)} async-done(((bf16[64,512]{1,0:T(8,128)(2,1)}), bf16[4096,512]{1,0:T(8,128)(2,1)}) %all-gather.13.cloned.1.call-update) | async-done | bytes 4194320 | tf_op jit(solution)/shard_map/all_gather | solution.py:38
  433.4 2.9 fusion.33
  437.0 111.6 %all-gather.21.cloned.1.call-done = bf16[8192,1,128]{0,2,1:T(8,128)(2,1)} async-done(((bf16[128,1,128]{0,2,1:T(8,128)(2,1)}), bf16[8192,1,128]{0,2,1:T(8,128)(2,1)}) %all-gather.21.cloned.1.call-update) | async-done | bytes 2097168 | tf_op jit(solution)/shard_map/all_gather | solution.py:84
  548.6 116.5 %all-gather.17.cloned.1.call-done = bf16[8192,128]{1,0:T(8,128)(2,1)} async-done(((bf16[128,128]{1,0:T(8,128)(2,1)}), bf16[8192,128]{1,0:T(8,128)(2,1)}) %all-gather.17.cloned.1.call-update) | async-done | bytes 2097168 | tf_op jit(solution)/shard_map/all_gather | solution.py:85
  665.1 145.2 %while.18 = (s32[]{:T(128)}, f32[1,512]{1,0:T(1,128)S(1)}, f32[1,512]{1,0:T(1,128)S(1)}, f32[1,512,128]{2,1,0:T(8,128)S(1)}, bf16[8192,128]{0,1:T(8,128)(2,1)}, ...) while((s32[]{:T(128)}, f32[1,512]{1,0:T(1,128)S(1)}, ...), condition=%wide.region_3.4_spmd.clone, body=%wide.region_0.3_spmd.clone.sunk | while | flops 34540164 | bytes 1551035 | solution.py:95
  666.2 1.1 fusion.55
  670.8 1.1 fusion.55
  684.4 1.1 fusion.55
  691.2 1.1 fusion.55
  695.7 1.1 fusion.55
  713.9 1.1 fusion.55
  716.2 1.1 fusion.55
  732.1 1.1 fusion.55
  754.8 1.1 fusion.55
  768.4 1.1 fusion.55
  791.1 1.1 fusion.55
  804.7 1.1 fusion.55
  810.6 4.7 convolution_convert_fusion
  815.3 89.9 %reduce-scatter.2.cloned.1.call-done = bf16[128,512]{1,0:T(8,128)(2,1)} async-done(((bf16[128,4096]{1,0:T(8,128)(2,1)}), bf16[128,512]{1,0:T(8,128)(2,1)}) %reduce-scatter.2.cloned.1.call-update) | async-done | bytes 131088 | tf_op jit(solution)/shard_map/reduce_scatter | solution.py:108
  (534 shorter events, 133.6 us)
Async XLA Ops:
  6.5 72.4 %all-gather.9.cloned.1.call-start = ((), (), s32[]{:S(2)}) async-start(), calls=%async_computation.1 | async-start | bytes 1179648 | tf_op jit(solution)/shard_map/all_gather | solution.py:31
  7.3 189.0 %all-gather.11.cloned.1.call-start = ((), (), s32[]{:S(2)}) async-start(), calls=%async_computation.2 | async-start | bytes 1064960 | tf_op jit(solution)/shard_map/all_gather | solution.py:39
  8.0 305.7 %all-gather.15.cloned.1.call-start = ((), (), s32[]{:S(2)}) async-start(), calls=%async_computation.4 | async-start | bytes 1064960 | tf_op jit(solution)/shard_map/all_gather | solution.py:40
  8.7 424.7 %all-gather.13.cloned.1.call-start = ((), (), s32[]{:S(2)}) async-start(), calls=%async_computation.3 | async-start | bytes 4259840 | tf_op jit(solution)/shard_map/all_gather | solution.py:38
  9.3 539.2 %all-gather.21.cloned.1.call-start = ((), (), s32[]{:S(2)}) async-start(), calls=%async_computation.8 | async-start | bytes 2129920 | tf_op jit(solution)/shard_map/all_gather | solution.py:84
  79.0 354.5 %copy-start = (bf16[128,4096]{1,0:T(8,128)(2,1)S(1)}, bf16[128,4096]{1,0:T(8,128)(2,1)}, u32[]{:S(2)}) copy-start(bf16[128,4096]{1,0:T(8,128)(2,1)} %all-gather.9.cloned.1.call-done) | copy-start | bytes 3145732
  199.2 465.9 %all-gather.17.cloned.1.call-start = ((), (), s32[]{:S(2)}) async-start(), calls=%async_computation.5 | async-start | bytes 2129920 | tf_op jit(solution)/shard_map/all_gather | solution.py:85
  316.3 494.3 %all-gather.19.cloned.1.call-start = ((), (), s32[]{:S(2)}) async-start(), calls=%async_computation.6 | async-start | bytes 4259840 | tf_op jit(solution)/shard_map/all_gather | solution.py:105
  317.1 588.2 %reduce-scatter.2.cloned.1.call-start = ((), (), s32[]{:S(2)}) async-start(), calls=%async_computation.7 | async-start | bytes 1179648 | tf_op jit(solution)/shard_map/reduce_scatter | solution.py:108
Sparse Core Ops, SparseCore 0:
  10.4 68.5 all-gather.8
  81.1 115.1 all-gather.10
  198.5 115.2 all-gather.14
  315.7 117.6 all-gather.12
  435.3 113.1 all-gather.20
  550.6 114.4 all-gather.16
  667.2 117.7 all-gather.18
  815.5 89.7 reduce-scatter.1
where the time goes:
time: 921 us; the launch traced here: 912 us
  waiting for transfers between devices  739 us (80%)
  matrix products  144 us (16%)
  between operations  13.6 us (1%)
  other arithmetic  10.8 us (1%)
    all_gather x1, waiting for transfers between devices, body(): key_sum = add_rows(lax.all_gather(key_matrix, 'ctx', axis=0, tiled=True))  117 us
    all_gather x1, waiting for transfers between devices, body(): value_piece = lax.all_gather(projected_values, 'ctx', axis=0, tiled=True)  117 us
    all_gather x1, waiting for transfers between devices, body(): query_sum = add_rows(lax.all_gather(w_query, 'ctx', axis=0, tiled=True))  116 us
    all_gather x1, waiting for transfers between devices, body(): lax.all_gather(value_matrix, 'ctx', axis=0, tiled=True)  114 us
    all_gather x1, waiting for transfers between devices, body(): key_piece = lax.all_gather(projected_keys, 'ctx', axis=0, tiled=True)  112 us
    reduce_scatter x1, waiting for transfers between devices, body(): lax.psum_scatter(partial_out.astype(jnp.bfloat16), 'fsdp', scatter_dimens...  89.9 us
    all_gather x1, waiting for transfers between devices, body(): features = lax.all_gather(tokens, 'fsdp', axis=1, tiled=True)  69.6 us
    dot_general x64, matrix products, update(): jnp.einsum('gqk,kgd->gqd', exp_weights.astype(jnp.bfloat16), value_heads,...  68.1 us
  transfers between devices with their start and end apart: 8, of which 7 were waited for; matrix products, arithmetic and copies ran while one was open for 16% of the time, Pallas kernels for 0%

commit v1 on v0

--- a/solution.py
+++ b/solution.py
@@ -82,7 +82,9 @@
         jnp.zeros((kv_heads, query_rows, HEAD_SIZE), jnp.float32),
     )
     key_piece = lax.all_gather(projected_keys, "ctx", axis=0, tiled=True)
-    value_piece = lax.all_gather(projected_values, "ctx", axis=0, tiled=True)
+    value_piece = jnp.concatenate(
+        lax.all_to_all(jnp.stack([projected_values] * lax.axis_size("ctx")), "ctx", 0, 0), axis=0
+    )
     block_rows = min(tok_count, key_piece.shape[0])
     block_count = key_piece.shape[0] // block_rows
 

time: 921 us -> 804 us (0.87)
  waiting for transfers between devices: 739 us -> 663 us
  matrix products: 144 us -> 95.3 us
    all_gather x1 -> x0, waiting for transfers between devices: 117 us -> none  [body(): value_piece = lax.all_gather(projected_values, 'ctx', axis=0, tiled=True)]
    dot_general x64, matrix products: 68.1 us -> 19.6 us  [update(): jnp.einsum('gqk,kgd->gqd', exp_weights.astype(jnp.bfloat16), value_heads,...]
    all_gather x1, waiting for transfers between devices: 0.02 us -> 21 us  [body(): lax.all_gather(w_out, 'ctx', axis=1, tiled=True)]
    all_gather x1, waiting for transfers between devices: 116 us -> 136 us  [body(): query_sum = add_rows(lax.all_gather(w_query, 'ctx', axis=0, tiled=True))]
  transfers between devices with their start and end apart: 8 -> 8, of which waited for: 7 -> 7; matrix products, arithmetic and copies ran while one was open for 16% -> 13% of each run, Pallas kernels for 0% -> 0%
where the time goes in v1:
time: 804 us; the launch traced here: 799 us
  waiting for transfers between devices  663 us (82%)
  matrix products  95.3 us (12%)
  between operations  13.6 us (2%)
  other arithmetic  11.4 us (1%)
    all_gather x1, waiting for transfers between devices, body(): query_sum = add_rows(lax.all_gather(w_query, 'ctx', axis=0, tiled=True))  136 us
    all_gather x1, waiting for transfers between devices, body(): key_sum = add_rows(lax.all_gather(key_matrix, 'ctx', axis=0, tiled=True))  117 us
    all_gather x1, waiting for transfers between devices, body(): lax.all_gather(value_matrix, 'ctx', axis=0, tiled=True)  115 us
    all_gather x1, waiting for transfers between devices, body(): key_piece = lax.all_gather(projected_keys, 'ctx', axis=0, tiled=True)  111 us
    reduce_scatter x1, waiting for transfers between devices, body(): lax.psum_scatter(partial_out.astype(jnp.bfloat16), 'fsdp', scatter_dimens...  90.5 us
    all_gather x1, waiting for transfers between devices, body(): features = lax.all_gather(tokens, 'fsdp', axis=1, tiled=True)  69.6 us
    dot_general x64, matrix products, update(): jnp.einsum('gqd,kgd->gqk', stacked, key_heads, preferred_element_type=jnp...  63.3 us
    all_gather x1, waiting for transfers between devices, body(): lax.all_gather(w_out, 'ctx', axis=1, tiled=True)  21 us
  transfers between devices with their start and end apart: 8, of which 7 were waited for; matrix products, arithmetic and copies ran while one was open for 13% of the time, Pallas kernels for 0%

profile of v1, /device:TPU:2, one launch (start us, length us, event | category | flops | bytes accessed | tf_op | source)
XLA Modules:
  0.0 799.0 jit_solution(15346242149463028472)
XLA Ops:
  9.4 69.6 %all-gather.8.cloned.1.call-done = bf16[128,4096]{1,0:T(8,128)(2,1)} async-done(((bf16[128,512]{1,0:T(8,128)(2,1)}), bf16[128,4096]{1,0:T(8,128)(2,1)}) %all-gather.8.cloned.1.call-update) | async-done | bytes 1048592 | tf_op jit(solution)/shard_map/all_gather | solution.py:31
  79.0 117.3 %all-gather.10.cloned.1.call-done = bf16[4096,128]{1,0:T(8,128)(2,1)} async-done(((bf16[64,128]{1,0:T(8,128)(2,1)}), bf16[4096,128]{1,0:T(8,128)(2,1)}) %all-gather.10.cloned.1.call-update) | async-done | bytes 1048592 | tf_op jit(solution)/shard_map/all_gather | solution.py:39
  196.3 2.1 convolution_bitcast_fusion.1
  199.2 114.5 %all-gather.14.cloned.1.call-done = bf16[4096,128]{1,0:T(8,128)(2,1)} async-done(((bf16[64,128]{1,0:T(8,128)(2,1)}), bf16[4096,128]{1,0:T(8,128)(2,1)}) %all-gather.14.cloned.1.call-update) | async-done | bytes 1048592 | tf_op jit(solution)/shard_map/all_gather | solution.py:40
  313.7 2.0 convolution_convert_fusion.1
  315.7 1.8 stack.2
  317.5 7.4 all-to-all-start
  326.6 136.4 %all-gather.12.cloned.1.call-done = bf16[4096,512]{1,0:T(8,128)(2,1)} async-done(((bf16[64,512]{1,0:T(8,128)(2,1)}), bf16[4096,512]{1,0:T(8,128)(2,1)}) %all-gather.12.cloned.1.call-update) | async-done | bytes 4194320 | tf_op jit(solution)/shard_map/all_gather | solution.py:38
  463.0 3.6 fusion.33
  466.7 1.0 reshape.206
  468.2 110.6 %all-gather.18.cloned.1.call-done = bf16[8192,1,128]{0,2,1:T(8,128)(2,1)} async-done(((bf16[128,1,128]{0,2,1:T(8,128)(2,1)}), bf16[8192,1,128]{0,2,1:T(8,128)(2,1)}) %all-gather.18.cloned.1.call-update) | async-done | bytes 2097168 | tf_op jit(solution)/shard_map/all_gather | solution.py:84
  578.8 96.8 %while.18 = (s32[]{:T(128)}, f32[1,512]{1,0:T(1,128)S(1)}, f32[1,512]{1,0:T(1,128)S(1)}, f32[1,512,128]{2,1,0:T(8,128)S(1)}, bf16[8192,128]{0,1:T(8,128)(2,1)}, ...) while((s32[]{:T(128)}, f32[1,512]{1,0:T(1,128)S(1)}, ...), condition=%wide.region_3.4_spmd.clone, body=%wide.region_0.3_spmd.clone.sunk | while | flops 34540164 | bytes 1551035 | solution.py:97
  590.9 1.0 fusion.51
  595.4 1.0 fusion.51
  601.5 1.0 fusion.51
  603.0 1.0 fusion.51
  604.5 1.0 fusion.51
  610.6 1.0 fusion.51
  643.9 1.0 fusion.51
  648.4 1.0 fusion.51
  651.4 1.0 fusion.51
  675.9 21.0 %all-gather.16.cloned.1.call-done = bf16[512,4096]{0,1:T(8,128)(2,1)} async-done(((bf16[512,64]{0,1:T(8,128)(2,1)}), bf16[512,4096]{0,1:T(8,128)(2,1)}) %all-gather.16.cloned.1.call-update) | async-done | bytes 4194320 | tf_op jit(solution)/shard_map/all_gather | solution.py:107
  696.9 4.7 convolution_convert_fusion
  701.6 90.5 %reduce-scatter.2.cloned.1.call-done = bf16[128,512]{1,0:T(8,128)(2,1)} async-done(((bf16[128,4096]{1,0:T(8,128)(2,1)}), bf16[128,512]{1,0:T(8,128)(2,1)}) %reduce-scatter.2.cloned.1.call-update) | async-done | bytes 131088 | tf_op jit(solution)/shard_map/reduce_scatter | solution.py:110
  (536 shorter events, 89.3 us)
Async XLA Ops:
  6.5 72.4 %all-gather.8.cloned.1.call-start = ((), (), s32[]{:S(2)}) async-start(), calls=%async_computation.2 | async-start | bytes 1179648 | tf_op jit(solution)/shard_map/all_gather | solution.py:31
  7.3 189.0 %all-gather.10.cloned.1.call-start = ((), (), s32[]{:S(2)}) async-start(), calls=%async_computation.3 | async-start | bytes 1064960 | tf_op jit(solution)/shard_map/all_gather | solution.py:39
  8.0 305.7 %all-gather.14.cloned.1.call-start = ((), (), s32[]{:S(2)}) async-start(), calls=%async_computation.5 | async-start | bytes 1064960 | tf_op jit(solution)/shard_map/all_gather | solution.py:40
  8.7 454.3 %all-gather.12.cloned.1.call-start = ((), (), s32[]{:S(2)}) async-start(), calls=%async_computation.4 | async-start | bytes 4259840 | tf_op jit(solution)/shard_map/all_gather | solution.py:38
  9.3 569.5 %all-gather.18.cloned.1.call-start = ((), (), s32[]{:S(2)}) async-start(), calls=%async_computation.8 | async-start | bytes 2129920 | tf_op jit(solution)/shard_map/all_gather | solution.py:84
  9.4 308.1 %copy-start.1 = (f32[128]{0:T(128)}, f32[128]{0:T(128)S(1)}, u32[]{:S(2)}) copy-start(f32[128]{0:T(128)S(1)} %fusion.31) | copy-start | bytes 1540
  199.2 263.8 %copy-start = (bf16[128,4096]{1,0:T(8,128)(2,1)S(1)}, bf16[128,4096]{1,0:T(8,128)(2,1)}, u32[]{:S(2)}) copy-start(bf16[128,4096]{1,0:T(8,128)(2,1)} %all-gather.8.cloned.1.call-done) | copy-start | bytes 3145732
  317.5 261.2 %all-to-all-start = ((bf16[64,128,128]{2,1,0:T(8,128)(2,1)}), bf16[64,128,128]{2,1,0:T(8,128)(2,1)S(1)}, u32[]{:S(2)}, u32[]{:S(2)}) async-start(bf16[64,128,128]{2,1,0:T(8,128)(2,1)} %stack.2), calls=%async_computation | async-start | bytes 4194304 | tf_op jit(solution)/shard_map/all_to_all | solution.py:86
  324.9 372.0 %all-gather.16.cloned.1.call-start = ((), (), s32[]{:S(2)}) async-start(), calls=%async_computation.6 | async-start | bytes 4259840 | tf_op jit(solution)/shard_map/all_gather | solution.py:107
  325.5 466.6 %reduce-scatter.2.cloned.1.call-start = ((), (), s32[]{:S(2)}) async-start(), calls=%async_computation.7 | async-start | bytes 1179648 | tf_op jit(solution)/shard_map/reduce_scatter | solution.py:110
Sparse Core Ops, SparseCore 0:
  10.4 68.5 all-gather.7
  81.1 115.1 all-gather.9
  198.5 115.2 all-gather.13
  315.7 147.2 all-gather.11
  464.9 113.8 all-gather.17
  580.8 116.0 all-gather.15
  701.7 90.3 reduce-scatter.1
